TPU v7x, 256 devices: a whole 4x4x8 slice. The times are simulated.
256 devices in a mesh: wide: 64 (over z, y, core), narrow: 4 (over x).
Axes of the slice: x: 4, y: 4, z: 8, core: 2. Of those that a mesh axis runs over, the one named last changes fastest.
Arguments:
- stored_amps: float32 [1024, 16384], P('wide', 'narrow'), may hold values from -6 to 6
- integrals: float32 [16384, 16384], P('narrow', 'wide'), may hold values from -0.046875 to 0.046875
- pair_counts: int32 [4], replicated, may hold values from 2048 to 4096, as said below
- block_map: int32 [64], replicated, may hold values from 0 to 63, each once
Outputs:
- cycle_out: float32 [1024, 16384], P('wide', 'narrow')
Inputs may be any that keep to these rules, and one draw needn't show every extreme that they name: `pair_counts`: each count lies between half of 4096 and 4096; one count equals 4096. `block_map`: a permutation of the indices of wide.
All inputs are finite; a program needn't handle non-finite values.
Results may differ from a plain program's by a relative error of at most 0.000086.
Values sent between devices are 32-bit elements; how exact they have to be, the bound alone decides.
No kernel may reach another device: no remote copies, remote signals or barrier semaphores. Data moves between devices by JAX's collectives and lax.ppermute only.
A program may use at most 64 MiB of HBM per device.

v0:
```python
import jax
import jax.numpy as jnp
from jax import lax
from jax.sharding import PartitionSpec as P

PB = 4096
BR = 8


def true_order(rows_block, block_map, count_wide):
    total = rows_block.shape[0]
    width = rows_block.shape[1]
    slots = total // (count_wide * BR)
    shaped = rows_block.reshape(count_wide, slots, BR, width)
    shaped = jnp.take(shaped, block_map, axis=0)
    return jnp.transpose(shaped, (1, 0, 2, 3)).reshape(total, width)


def on_device(stored_amps, integrals, pair_counts, block_map):
    count_wide = lax.axis_size("wide")
    count_narrow = lax.axis_size("narrow")
    layer = lax.axis_index("narrow")
    width = stored_amps.shape[1]
    columns = layer * width + jnp.arange(width, dtype=jnp.int32)
    owner = columns // PB
    limit = jnp.sum(
        jnp.where(
            owner[:, None] == jnp.arange(4, dtype=jnp.int32)[None, :], pair_counts[None, :], 0
        ),
        axis=1,
    )
    masked = jnp.where((columns % PB < limit)[None, :], stored_amps, jnp.float32(0.0))
    local_cols = integrals.shape[1]
    cycle = jnp.dot(
        lax.all_gather(masked, "wide", axis=0, tiled=True),
        integrals,
        precision=lax.Precision.HIGHEST,
        preferred_element_type=jnp.float32,
    )
    ordered = true_order(cycle, block_map, count_wide)
    moved = lax.all_to_all(ordered, "wide", split_axis=0, concat_axis=1, tiled=True)
    height = moved.shape[0]
    group = local_cols // count_narrow
    moved = moved.reshape(height, count_wide, count_narrow, group)
    moved = jnp.transpose(moved, (0, 2, 1, 3)).reshape(height, count_wide * local_cols)
    cycle_out = lax.psum_scatter(moved, "narrow", scatter_dimension=1, tiled=True)
    return cycle_out


def solution(mesh):
    placed = (P("wide", "narrow"), P("narrow", "wide"), P(), P())
    return jax.shard_map(
        on_device, mesh=mesh, in_specs=placed, out_specs=P("wide", "narrow"), check_vma=False
    )
```

profile of v0, /device:TPU:8, one launch (start us, length us, event | category | flops | bytes accessed | tf_op | source)
XLA Modules:
  0.0 200.3 jit_solution(17723670310562345288)
XLA Ops:
  6.5 0.0 all-gather.2.cloned.1.call-start
  6.6 0.8 select_reduce_fusion
  7.4 1.7 broadcast_select_fusion
  9.0 0.0 all-gather.2.cloned.1.call-update
  9.1 0.0 reduce-scatter.2.cloned.1.call-start
  9.1 0.7 compare_select_fusion
  9.8 0.7 compare_and_fusion
  10.4 100.6 %all-gather.2.cloned.1.call-done = f32[1024,4096]{1,0:T(8,128)} async-done(((f32[16,4096]{1,0:T(8,128)}), f32[1024,4096]{1,0:T(8,128)}) %all-gather.2.cloned.1.call-update) | async-done | bytes 16777232 | tf_op jit(solution)/shard_map/all_gather | solution.py:35
  111.0 16.2 %fusion.6 = f32[1024,256]{1,0:T(8,128)S(1)} fusion(f32[1024,4096]{1,0:T(8,128)} %all-gather.2.cloned.1.call-done, f32[4096,256]{1,0:T(8,128)} %param.5), kind=kOutput, calls=%fused_computation.21 | convolution fusion | flops 12884901888 | bytes 22020096 | tf_op jit(solution)/shard_map/dot_general | solution.py:34
  127.2 0.6 gather_fusion
  127.9 0.1 select_bitcast_fusion
  128.0 0.1 copy.9
  128.1 36.1 %all_to_all.16 = f32[64,16,256]{2,1,0:T(8,128)S(1)} all-to-all(f32[64,16,256]{2,1,0:T(8,128)S(1)} %bitcast.11), channel_id=1, replica_groups=mesh['wide'=64,'narrow'=4] {'wide'}, dimensions={0} | all-to-all | bytes 2097152 | tf_op jit(solution)/shard_map/all_to_all | solution.py:41
  164.2 0.6 copy.10
  164.8 0.9 reshape.59
  165.7 1.7 copy.11
  167.4 3.2 %reshape.60 = f32[16,16384]{1,0:T(8,128)} reshape(f32[16,4,64,64]{3,2,1,0:T(8,128)} %copy.11) | data formatting | bytes 2097152 | tf_op jit(solution)/shard_map/reshape | solution.py:45
  170.6 0.0 reduce-scatter.2.cloned.1.call-update
  170.6 22.9 %reduce-scatter.2.cloned.1.call-done = f32[16,4096]{1,0:T(8,128)} async-done(((f32[16,16384]{1,0:T(8,128)}), f32[16,4096]{1,0:T(8,128)}) %reduce-scatter.2.cloned.1.call-update) | async-done | bytes 262160 | tf_op jit(solution)/shard_map/reduce_scatter | solution.py:46
  (3 shorter events, 0.0 us)
Async XLA Ops:
  6.5 104.5 %all-gather.2.cloned.1.call-start = ((), (), s32[]{:S(2)}) async-start(), calls=%async_computation.2 | async-start | bytes 17039360 | tf_op jit(solution)/shard_map/all_gather | solution.py:35
  9.1 184.4 %reduce-scatter.2.cloned.1.call-start = ((), (), s32[]{:S(2)}) async-start(), calls=%async_computation.3 | async-start | bytes 1310720 | tf_op jit(solution)/shard_map/reduce_scatter | solution.py:46
Sparse Core Ops, SparseCore 0:
  10.1 100.8 all-gather.1
  170.7 22.6 reduce-scatter.1
where the time goes:
time: 201 us; the launch traced here: 200 us
  waiting for transfers between devices  123 us (61%)
  blocking collectives  36.1 us (18%)
  matrix products  16.2 us (8%)
  between operations  13.5 us (7%)
  local copies, waits for them, and re-layouts  7.09 us (4%)
  other arithmetic  3.96 us (2%)
    all_gather x1, waiting for transfers between devices, on_device(): lax.all_gather(masked, 'wide', axis=0, tiled=True)  101 us
    all_to_all x1, blocking collectives, on_device(): lax.all_to_all(ordered, 'wide', split_axis=0, concat_axis=1, tiled=True)  36.1 us
    reduce_scatter x1, waiting for transfers between devices, on_device(): lax.psum_scatter(moved, 'narrow', scatter_dimension=1, tiled=True)  22.9 us
    dot_general x1, matrix products, on_device(): jnp.dot(lax.all_gather(masked, 'wide', axis=0, tiled=True), integrals, pr...  16.2 us
  transfers between devices with their start and end apart: 2, of which 2 were waited for; matrix products, arithmetic and copies ran while one was open for 1% of the time, Pallas kernels for 0%

commit v1 on v0

v1 whole, which is shorter than its diff:
```python
import jax
import jax.numpy as jnp
import numpy as np
from jax import lax
from jax.sharding import Mesh
from jax.sharding import PartitionSpec as P

PB = 4096
BR = 8


def on_device(stored_amps, integrals, pair_counts, block_map):
    core = lax.axis_index("core")
    layer = lax.axis_index("x")
    nx = lax.axis_size("x")
    width = stored_amps.shape[1]
    rows = stored_amps.shape[0]
    chips = lax.axis_size("z") * lax.axis_size("y")
    depth, cols = integrals.shape
    group = cols // nx
    limit = lax.dynamic_index_in_dim(pair_counts, layer * width // PB, keepdims=False)
    column = lax.broadcasted_iota(jnp.int32, (rows, width), 1)
    masked = jnp.where(column < limit, stored_amps, jnp.float32(0.0))
    gathered = lax.all_gather(masked, ("z", "y"), axis=0, tiled=True)
    swap = [(0, 1), (1, 0)]
    other = lax.ppermute(integrals, "core", swap)
    mine = integrals.reshape(depth, nx, group)
    other = other.reshape(depth, nx, group)
    pair = jnp.concatenate(
        [jnp.where(core == 0, mine, other), jnp.where(core == 0, other, mine)], axis=2
    )
    pair = pair.reshape(depth, nx * 2 * group)
    both = jnp.dot(
        gathered, pair, precision=lax.Precision.HIGH, preferred_element_type=jnp.float32
    )
    total = lax.dynamic_slice_in_dim(both, layer * 2 * group, 2 * group, axis=1)
    for step in (1, 3, 2):
        to = (layer + step) % nx
        part = lax.dynamic_slice_in_dim(both, to * 2 * group, 2 * group, axis=1)
        total = total + lax.ppermute(part, "x", [(i, (i + step) % nx) for i in range(nx)])
    partner = lax.ppermute(total, "core", swap)
    blocks = jnp.concatenate([total, partner], axis=0).reshape(-1, BR, 2 * group)
    target = 2 * jnp.arange(chips, dtype=jnp.int32) + core
    slot = target // chips
    first = 2 * (target % chips)
    owner = jnp.take(block_map, jnp.stack([first, first + 1], axis=1).reshape(-1), axis=0)
    where_is = jnp.where(owner % 2 != core, chips, 0) + owner // 2
    index = where_is * 2 + jnp.repeat(slot, 2)
    chosen = jnp.take(blocks, index, axis=0).reshape(chips, rows, 2 * group)
    moved = lax.all_to_all(chosen, ("z", "y"), split_axis=0, concat_axis=0, tiled=True)
    return jnp.transpose(moved, (1, 0, 2)).reshape(rows, chips * 2 * group)


def solution(mesh):
    fine = Mesh(np.asarray(mesh.devices).reshape(8, 4, 2, 4), ("z", "y", "core", "x"))
    wide = ("z", "y", "core")
    placed = (P(wide, "x"), P("x", wide), P(), P())
    return jax.shard_map(
        on_device, mesh=fine, in_specs=placed, out_specs=P(wide, "x"), check_vma=False
    )
```

time: 201 us -> 166 us (0.83)
  waiting for transfers between devices: 123 us -> 95.9 us
  blocking collectives: 36.1 us -> 18.5 us
  other arithmetic: 3.96 us -> 10.8 us
  matrix products: 16.2 us -> 10.4 us
  starting transfers between devices: 0.04 us -> 5.18 us
  local copies, waits for them, and re-layouts: 7.09 us -> 9.79 us
    reduce_scatter x1 -> x0, waiting for transfers between devices: 22.9 us -> none  [on_device(): lax.psum_scatter(moved, 'narrow', scatter_dimension=1, tiled=True)]
    all_gather x1, waiting for transfers between devices: 101 us -> 78.4 us  [on_device(): gathered = lax.all_gather(masked, ('z', 'y'), axis=0, tiled=True)]
    all_to_all x1, blocking collectives: 36.1 us -> 18.5 us  [on_device(): lax.all_to_all(chosen, ('z', 'y'), split_axis=0, concat_axis=0, tiled=True)]
    ppermute x0 -> x5, waiting for transfers between devices: none -> 17.4 us  [the longest x3 9.61 us: on_device(): lax.ppermute(part, 'x', [(i, (i + step) % nx) for i in range(nx)])]
    dot_general x1, matrix products: 16.2 us -> 10.4 us  [on_device(): jnp.dot(gathered, pair, precision=lax.Precision.HIGH, preferred_element_t...]
    unnamed x0 -> x3, local copies, waits for them, and re-layouts: none -> 5.64 us
    ppermute x0 -> x5, starting transfers between devices: none -> 5.18 us  [the longest x3 5.08 us: on_device(): lax.ppermute(part, 'x', [(i, (i + step) % nx) for i in range(nx)])]
    concatenate x0 -> x1, other arithmetic: none -> 3.78 us  [on_device(): jnp.concatenate([jnp.where(core == 0, mine, other), jnp.where(core == 0,...]
  transfers between devices with their start and end apart: 2 -> 6, of which waited for: 2 -> 6; matrix products, arithmetic and copies ran while one was open for 1% -> 9% of each run, Pallas kernels for 0% -> 0%
where the time goes in v1:
time: 166 us; the launch traced here: 164 us
  waiting for transfers between devices  95.9 us (58%)
  blocking collectives  18.5 us (11%)
  between operations  13.5 us (8%)
  other arithmetic  10.8 us (7%)
  matrix products  10.4 us (6%)
  local copies, waits for them, and re-layouts  9.79 us (6%)
  starting transfers between devices  5.18 us (3%)
    all_gather x1, waiting for transfers between devices, on_device(): gathered = lax.all_gather(masked, ('z', 'y'), axis=0, tiled=True)  78.4 us
    all_to_all x1, blocking collectives, on_device(): lax.all_to_all(chosen, ('z', 'y'), split_axis=0, concat_axis=0, tiled=True)  18.5 us
    dot_general x1, matrix products, on_device(): jnp.dot(gathered, pair, precision=lax.Precision.HIGH, preferred_element_t...  10.4 us
    ppermute x3, waiting for transfers between devices, on_device(): lax.ppermute(part, 'x', [(i, (i + step) % nx) for i in range(nx)])  9.61 us
    ppermute x1, waiting for transfers between devices, on_device(): other = lax.ppermute(integrals, 'core', swap)  6.32 us
    unnamed x3, local copies, waits for them, and re-layouts  5.64 us
    ppermute x3, starting transfers between devices, on_device(): lax.ppermute(part, 'x', [(i, (i + step) % nx) for i in range(nx)])  5.08 us
    select_n x1, other arithmetic, on_device(): jnp.where(core == 0, mine, other)  4.29 us
  transfers between devices with their start and end apart: 6, of which 6 were waited for; matrix products, arithmetic and copies ran while one was open for 9% of the time, Pallas kernels for 0%

profile of v1, /device:TPU:8, one launch (start us, length us, event | category | flops | bytes accessed | tf_op | source)
XLA Modules:
  0.0 164.1 jit_solution(13453872497349946249)
XLA Ops:
  6.5 0.0 copy-start
  6.5 0.0 all-gather.2.cloned.1.call-start
  6.5 1.2 dynamic_slice.16
  7.8 0.7 iota_compare_fusion
  8.4 1.7 %broadcast_select_fusion.2 = f32[16,4096]{1,0:T(8,128)} fusion(f32[16,4096]{1,0:T(8,128)} %param.4, pred[4096]{0:T(1024)(128)(4,1)S(1)} %iota_compare_fusion), kind=kLoop, calls=%fused_computation.9 | loop fusion | flops 65536 | bytes 528384 | tf_op jit(solution)/shard_map/jit(_where)/select_n | solution.py:23
  10.1 0.0 all-gather.2.cloned.1.call-update
  10.2 5.6 %copy.26 = f32[4096,256]{0,1:T(8,128)} copy(f32[4096,256]{1,0:T(8,128)} %param.5) | data formatting | bytes 8388608 | tf_op args[1]
  15.8 0.0 collective-permute-start
  15.8 0.1 copy.19
  15.9 0.1 reshape.241
  16.0 0.0 copy-done
  16.0 0.8 gather_fusion
  16.8 0.1 gather.15
  17.0 6.3 %collective-permute-done = f32[4096,256]{0,1:T(8,128)} collective-permute-done((f32[4096,256]{0,1:T(8,128)}, f32[4096,256]{0,1:T(8,128)}, u32[]{:S(2)}, u32[]{:S(2)}) %collective-permute-start) | collective-permute-done | bytes 4194336 | tf_op jit(solution)/shard_map/ppermute | solution.py:26
  23.3 4.3 %broadcast_select_fusion.1 = (f32[4096,256]{0,1:T(8,128)S(1)}, f32[4096,256]{0,1:T(8,128)S(1)}) fusion(f32[4096,256]{0,1:T(8,128)} %copy.26, f32[4096,256]{0,1:T(8,128)} %collective-permute-done, pred[]{:T(512)S(6)} %eq.12), kind=kLoop, calls=%fused_computation.4 | loop fusion | flops 2097152 | bytes 16777216 | tf_op jit(solution)/shard_map/jit(_where)/select_n | solution.py:30
  27.6 3.8 %pad_maximum_fusion = f32[4096,4,128]{0,2,1:T(8,128)} fusion(f32[4096,4,64]{0,2,1:T(8,128)S(1)} %bitcast.28, f32[4096,4,64]{0,2,1:T(8,128)S(1)} %bitcast.27), kind=kLoop, calls=%fused_computation.2 | loop fusion | flops 2097152 | bytes 16777216 | tf_op jit(solution)/shard_map/concatenate | solution.py:29
  31.4 78.4 %all-gather.2.cloned.1.call-done = f32[512,4096]{1,0:T(8,128)} async-done(((f32[16,4096]{1,0:T(8,128)}), f32[512,4096]{1,0:T(8,128)}) %all-gather.2.cloned.1.call-update) | async-done | bytes 8388624 | tf_op jit(solution)/shard_map/all_gather | solution.py:24
  109.8 10.4 %fusion.11 = f32[512,512]{1,0:T(8,128)S(1)} fusion(f32[512,4096]{1,0:T(8,128)} %all-gather.2.cloned.1.call-done, f32[4096,512]{0,1:T(8,128)} %bitcast.29), kind=kOutput, calls=%fused_computation.55 | convolution fusion | flops 6442450944 | bytes 17825792 | tf_op jit(solution)/shard_map/dot_general | solution.py:33
  120.2 0.1 constant_dynamic-slice_fusion.2
  120.4 1.5 collective-permute-start.1
  121.9 1.8 %collective-permute-start.2 = (f32[512,128]{1,0:T(8,128)S(1)}, f32[512,128]{1,0:T(8,128)S(1)}, u32[]{:S(2)}, u32[]{:S(2)}) collective-permute-start(f32[512,128]{1,0:T(8,128)S(1)} %get-tuple-element.9), channel_id=1, source_target_pairs={{0,3},{1,0},{2,1},{3,2},{4,7},{5,4},{6,5},{7,6},{8,11},{9,8},{10,9... | collective-permute-start | bytes 786440 | tf_op jit(solution)/shard_map/ppermute | solution.py:40
  123.7 1.8 %collective-permute-start.3 = (f32[512,128]{1,0:T(8,128)S(1)}, f32[512,128]{1,0:T(8,128)S(1)}, u32[]{:S(2)}, u32[]{:S(2)}) collective-permute-start(f32[512,128]{1,0:T(8,128)S(1)} %get-tuple-element.8), channel_id=1, source_target_pairs={{0,2},{1,3},{2,0},{3,1},{4,6},{5,7},{6,4},{7,5},{8,10},{9,11},{10,... | collective-permute-start | bytes 786440 | tf_op jit(solution)/shard_map/ppermute | solution.py:40
  125.4 0.1 compare_and_fusion
  125.5 0.1 broadcast_in_dim.39
  125.6 0.1 reshape.244
  125.7 0.1 copy.23
  125.8 0.1 copy.24
  125.9 4.0 %collective-permute-done.1 = f32[512,128]{1,0:T(8,128)S(1)} collective-permute-done((f32[512,128]{1,0:T(8,128)S(1)}, f32[512,128]{1,0:T(8,128)S(1)}, u32[]{:S(2)}, u32[]{:S(2)}) %collective-permute-start.1) | collective-permute-done | bytes 262176 | tf_op jit(solution)/shard_map/ppermute | solution.py:40
  129.9 4.0 %collective-permute-done.2 = f32[512,128]{1,0:T(8,128)S(1)} collective-permute-done((f32[512,128]{1,0:T(8,128)S(1)}, f32[512,128]{1,0:T(8,128)S(1)}, u32[]{:S(2)}, u32[]{:S(2)}) %collective-permute-start.2) | collective-permute-done | bytes 262176 | tf_op jit(solution)/shard_map/ppermute | solution.py:40
  133.9 1.6 collective-permute-done.3
  135.5 0.1 add_add_fusion
  135.6 0.1 collective-permute-start.4
  135.7 1.5 collective-permute-done.4
  137.2 0.6 gather_fusion.1
  137.9 0.1 bitcast_select_fusion
  138.0 18.5 %all_to_all.5 = f32[32,16,128]{2,1,0:T(8,128)S(1)} all-to-all(f32[32,16,128]{2,1,0:T(8,128)S(1)} %bitcast_select_fusion), channel_id=1, replica_groups=mesh['z'=8,'y'=4,'core'=2,'x'=4] {'z','y'}, dimensions={0} | all-to-all | bytes 524288 | tf_op jit(solution)/shard_map/all_to_all | solution.py:50
  156.5 0.7 copy_bitcast_fusion
  (9 shorter events, 0.1 us)
Async XLA Ops:
  6.5 9.5 %copy-start = (s32[64]{0:T(128)S(1)}, s32[64]{0:T(128)}, u32[]{:S(2)}) copy-start(s32[64]{0:T(128)} %param.7) | copy-start | bytes 772
  6.5 103.3 %all-gather.2.cloned.1.call-start = ((), (), s32[]{:S(2)}) async-start(), calls=%async_computation.1 | async-start | bytes 8650752 | tf_op jit(solution)/shard_map/all_gather | solution.py:24
  15.8 7.5 %collective-permute-start = (f32[4096,256]{0,1:T(8,128)}, f32[4096,256]{0,1:T(8,128)}, u32[]{:S(2)}, u32[]{:S(2)}) collective-permute-start(f32[4096,256]{0,1:T(8,128)} %copy.26), channel_id=1, source_target_pairs={{0,4},{4,0},{1,5},{5,1},{2,6},{6,2},{3,7},{7,3},{8,12},{12,8},{9,1... | collective-permute-start | bytes 12582920 | tf_op jit(solution)/shard_map/ppermute | solution.py:26
  120.4 9.5 %collective-permute-start.1 = (f32[512,128]{1,0:T(8,128)S(1)}, f32[512,128]{1,0:T(8,128)S(1)}, u32[]{:S(2)}, u32[]{:S(2)}) collective-permute-start(f32[512,128]{1,0:T(8,128)S(1)} %get-tuple-element.7), channel_id=1, source_target_pairs={{0,1},{1,2},{2,3},{3,0},{4,5},{5,6},{6,7},{7,4},{8,9},{9,10},{10,1... | collective-permute-start | bytes 786440 | tf_op jit(solution)/shard_map/ppermute | solution.py:40
  121.9 12.0 %collective-permute-start.2 = (f32[512,128]{1,0:T(8,128)S(1)}, f32[512,128]{1,0:T(8,128)S(1)}, u32[]{:S(2)}, u32[]{:S(2)}) collective-permute-start(f32[512,128]{1,0:T(8,128)S(1)} %get-tuple-element.9), channel_id=1, source_target_pairs={{0,3},{1,0},{2,1},{3,2},{4,7},{5,4},{6,5},{7,6},{8,11},{9,8},{10,9... | collective-permute-start | bytes 786440 | tf_op jit(solution)/shard_map/ppermute | solution.py:40
  123.7 11.8 %collective-permute-start.3 = (f32[512,128]{1,0:T(8,128)S(1)}, f32[512,128]{1,0:T(8,128)S(1)}, u32[]{:S(2)}, u32[]{:S(2)}) collective-permute-start(f32[512,128]{1,0:T(8,128)S(1)} %get-tuple-element.8), channel_id=1, source_target_pairs={{0,2},{1,3},{2,0},{3,1},{4,6},{5,7},{6,4},{7,5},{8,10},{9,11},{10,... | collective-permute-start | bytes 786440 | tf_op jit(solution)/shard_map/ppermute | solution.py:40
  135.6 1.6 collective-permute-start.4
Sparse Core Ops, SparseCore 0:
  10.3 99.4 all-gather.1
